TPU v7x, 32 devices: a whole 2x2x4 slice. The times are simulated.
32 devices in a mesh: rep: 8 (over y, x, core), tp: 4 (over z).
Axes of the slice: x: 2, y: 2, z: 4, core: 2. Of those that a mesh axis runs over, the one named last changes fastest.
Arguments:
- context: bfloat16 [16384, 5120], P('rep', 'tp'), may hold values from -6 to 6
- out_grad: bfloat16 [16384, 5120], P('rep', 'tp'), may hold values from -6 to 6
- rewards: int32 [8, 32], P(None, 'rep'), may hold values from 0 to 1
- master: float32 [5120, 5120], P('rep', 'tp'), may hold values from -0.078125 to 0.078125
- first_moment: float32 [5120, 5120], P('rep', 'tp'), may hold values from -0.046875 to 0.046875
- second_moment: float32 [5120, 5120], P('rep', 'tp'), may hold values from 6.1035155e-07 to 6.1035156e-05
- inputs: bfloat16 [4, 256, 5120], P(None, 'rep'), may hold values from -6 to 6
- w_query: bfloat16 [5120, 5120], P(None, 'tp'), may hold values from -0.078125 to 0.078125
- w_key: bfloat16 [5120, 1024], P(None, 'tp'), may hold values from -0.078125 to 0.078125
- w_value: bfloat16 [5120, 1024], P(None, 'tp'), may hold values from -0.078125 to 0.078125
- cache_keys: bfloat16 [256, 256, 1024], P('rep', None, 'tp'), may hold values from -400 to 400
- cache_values: bfloat16 [256, 256, 1024], P('rep', None, 'tp'), may hold values from -24 to 24
- lengths: int32 [32], P('rep'), may hold values from 64 to 256
Outputs:
- decoded: bfloat16 [4, 256, 5120], P(None, 'rep')
- adam_step: float32 [5120, 5120], P('rep', 'tp')
All inputs are finite; a program needn't handle non-finite values.
Results may differ from a plain program's by a relative error of at most 0.0088.
Values may be sent and summed in bfloat16 or wider, within the bound.
No kernel may reach another device: no remote copies, remote signals or barrier semaphores. Data moves between devices by JAX's collectives and lax.ppermute only.
A program may use at most 192 MiB of HBM per device.

v0:
```python
import jax
import jax.numpy as jnp
from jax import lax
from jax.sharding import PartitionSpec as P

HEAD_DIM = 128


rope_base = 1000000.0
first_beta = 0.9
second_beta = 0.95
adam_epsilon = 1e-08
step_count = 10
learn_rate = 0.001


def rotate(vectors, positions):
    half_dim = vectors.shape[-1] // 2
    frequency = rope_base ** (-2.0 * jnp.arange(half_dim, dtype=jnp.float32) / vectors.shape[-1])
    angles = positions[..., None].astype(jnp.float32) * frequency
    cosine_table = jnp.cos(angles)
    sine_table = jnp.sin(angles)
    former = vectors[..., :half_dim]
    latter = vectors[..., half_dim:]
    return jnp.concatenate(
        [former * cosine_table - latter * sine_table, latter * cosine_table + former * sine_table],
        axis=-1,
    )


def attend(queries, old_keys, old_values, new_keys, new_values, live_mask):
    score_scale = HEAD_DIM ** (-0.5)
    step_total = queries.shape[0]
    cache_scores = (
        jnp.einsum("tsgqd,scgd->tsgqc", queries, old_keys, preferred_element_type=jnp.float32)
        * score_scale
    )
    cache_scores = jnp.where(live_mask[None, :, None, None, :], cache_scores, -1e30)
    recent = (
        jnp.einsum("tsgqd,usgd->tsgqu", queries, new_keys, preferred_element_type=jnp.float32)
        * score_scale
    )
    causal = jnp.arange(step_total)[:, None] >= jnp.arange(step_total)[None, :]
    recent = jnp.where(causal[:, None, None, None, :], recent, -1e30)
    row_peak = jnp.maximum(jnp.max(cache_scores, axis=-1), jnp.max(recent, axis=-1))[..., None]
    cache_exp = jnp.exp(cache_scores - row_peak)
    recent_exp = jnp.exp(recent - row_peak)
    denominator = jnp.sum(cache_exp, axis=-1, keepdims=True) + jnp.sum(
        recent_exp, axis=-1, keepdims=True
    )
    cache_weight = (cache_exp / denominator).astype(jnp.bfloat16)
    recent_weight = (recent_exp / denominator).astype(jnp.bfloat16)
    attended = jnp.einsum(
        "tsgqc,scgd->tsgqd", cache_weight, old_values, preferred_element_type=jnp.float32
    )
    attended = attended + jnp.einsum(
        "tsgqu,usgd->tsgqd", recent_weight, new_values, preferred_element_type=jnp.float32
    )
    return attended.astype(jnp.bfloat16)


def per_device(
    context,
    out_grad,
    rewards,
    master,
    first_moment,
    second_moment,
    inputs,
    w_query,
    w_key,
    w_value,
    cache_keys,
    cache_values,
    lengths,
):
    replicas = lax.axis_size("rep")
    prompt_count, local_group = rewards.shape
    totals = lax.psum(jnp.sum(rewards, axis=1), "rep")
    group_size = local_group * replicas
    advantage = rewards.astype(jnp.float32) - totals.astype(jnp.float32)[:, None] / group_size
    token_local = context.shape[0]
    per_token = jnp.repeat(advantage.reshape(-1), token_local // (prompt_count * local_group)) / (
        token_local * replicas
    )
    scaled = (out_grad.astype(jnp.float32) * per_token[:, None]).astype(jnp.bfloat16)
    features = lax.all_gather(context, "tp", axis=1, tiled=True)
    gradient = lax.psum_scatter(
        lax.dot_general(
            features, scaled, (((0,), (0,)), ((), ())), preferred_element_type=jnp.float32
        ).astype(jnp.bfloat16),
        "rep",
        scatter_dimension=0,
        tiled=True,
    ).astype(jnp.float32)
    moment_new = first_beta * first_moment + (1.0 - first_beta) * gradient
    square_new = second_beta * second_moment + (1.0 - second_beta) * gradient * gradient
    adam_step = (
        moment_new
        / (1.0 - first_beta**step_count)
        / (jnp.sqrt(square_new / (1.0 - second_beta**step_count)) + adam_epsilon)
    )
    weight = (master - learn_rate * adam_step).astype(jnp.bfloat16)
    step_total, seq_local, model_width = inputs.shape
    local_heads = w_query.shape[1] // HEAD_DIM
    local_kv = w_key.shape[1] // HEAD_DIM
    flat_rows = inputs.reshape(step_total * seq_local, model_width)
    queries = jnp.dot(flat_rows, w_query, preferred_element_type=jnp.float32).reshape(
        step_total, seq_local, local_heads, HEAD_DIM
    )
    key_new = jnp.dot(flat_rows, w_key, preferred_element_type=jnp.float32).reshape(
        step_total, seq_local, local_kv, HEAD_DIM
    )
    value_new = (
        jnp.dot(flat_rows, w_value, preferred_element_type=jnp.float32)
        .reshape(step_total, seq_local, local_kv, HEAD_DIM)
        .astype(jnp.bfloat16)
    )
    seq_length = jnp.repeat(lengths, seq_local // lengths.shape[0])
    positions = seq_length[None, :] + jnp.arange(step_total, dtype=jnp.int32)[:, None]
    queries = rotate(queries, positions[:, :, None]).astype(jnp.bfloat16)
    queries = queries.reshape(step_total, seq_local, local_kv, local_heads // local_kv, HEAD_DIM)
    key_new = rotate(key_new, positions[:, :, None]).astype(jnp.bfloat16)
    slot_total = cache_keys.shape[1]
    old_keys = cache_keys.reshape(seq_local, slot_total, local_kv, HEAD_DIM)
    old_values = cache_values.reshape(seq_local, slot_total, local_kv, HEAD_DIM)
    live_mask = jnp.arange(slot_total, dtype=jnp.int32)[None, :] < seq_length[:, None]
    attended = attend(queries, old_keys, old_values, key_new, value_new, live_mask)
    attended = attended.reshape(step_total * seq_local, local_heads * HEAD_DIM)
    all_heads = lax.all_gather(attended, "tp", axis=1, tiled=True)
    feature_rows = lax.all_to_all(all_heads, "rep", split_axis=1, concat_axis=0, tiled=True)
    own_columns = lax.psum_scatter(
        jnp.dot(feature_rows, weight, preferred_element_type=jnp.float32),
        "rep",
        scatter_dimension=0,
        tiled=True,
    )
    decoded = lax.all_gather(own_columns.astype(jnp.bfloat16), "tp", axis=1, tiled=True)
    return (decoded.reshape(step_total, seq_local, model_width), adam_step)


def solution(mesh):
    placed = (
        P("rep", "tp"),
        P("rep", "tp"),
        P(None, "rep"),
        P("rep", "tp"),
        P("rep", "tp"),
        P("rep", "tp"),
        P(None, "rep", None),
        P(None, "tp"),
        P(None, "tp"),
        P(None, "tp"),
        P("rep", None, "tp"),
        P("rep", None, "tp"),
        P("rep"),
    )
    return jax.shard_map(
        per_device,
        mesh=mesh,
        in_specs=placed,
        out_specs=(P(None, "rep", None), P("rep", "tp")),
        check_vma=False,
    )
```

profile of v0, /device:TPU:0, one launch (start us, length us, event | category | flops | bytes accessed | tf_op | source)
XLA Modules:
  0.0 632.1 jit_solution(17506920975322697041)
XLA Ops:
  7.2 0.7 all-gather.6.cloned.1.call-update
  8.1 0.1 lt.20
  8.1 4.4 copy.64
  12.5 4.5 copy.69
  17.0 7.3 %reshape.131 = bf16[32,256,2,128]{3,2,1,0:T(2,128)(2,1)} reshape(bf16[32,256,256]{2,1,0:T(8,128)(2,1)} %param.23) | data formatting | bytes 8388608 | tf_op jit(solution)/shard_map/reshape | solution.py:125
  24.3 7.2 %reshape.132 = bf16[32,256,2,128]{3,2,1,0:T(2,128)(2,1)} reshape(bf16[32,256,256]{2,1,0:T(8,128)(2,1)} %param.24) | data formatting | bytes 8388608 | tf_op jit(solution)/shard_map/reshape | solution.py:126
  31.5 17.8 %copy.41 = bf16[5120,1280]{0,1:T(8,128)(2,1)} copy(bf16[5120,1280]{1,0:T(8,128)(2,1)} %param.20) | data formatting | bytes 26214400 | tf_op args[7]
  49.3 0.3 multiply_cosine_fusion
  49.6 7.2 %fusion.27 = f32[4,32,10,128]{3,1,2,0:T(8,128)S(1)} fusion(bf16[10,128,5120,1]{2,1,0,3:T(8,128)(2,1)} %bitcast.73, bf16[4,32,5120]{2,1,0:T(8,128)(2,1)S(1)} %copy-done), kind=kOutput, calls=%fused_computation.34 | convolution fusion | flops 1677721600 | bytes 15073280 | tf_op jit(solution)/shard_map/dot_general | solution.py:108
  56.9 0.3 subtract_convert_fusion.2
  57.1 0.2 copy.43
  57.3 0.2 copy.42
  57.5 1.1 copy-done.5
  58.6 1.0 fusion.25
  59.6 0.1 subtract_convert_fusion.3
  59.7 0.1 maximum_bitcast_fusion
  59.8 0.1 iota_compare_fusion
  59.9 2.6 fusion.55
  62.5 1.6 bitcast_reduce_fusion
  64.1 0.5 fusion.45
  64.6 1.3 fusion.16
  66.0 1.0 fusion.37
  67.0 0.5 convolution_bitcast_fusion
  67.5 0.7 copy-done.3
  68.2 1.5 fusion.29
  69.6 0.1 copy.50
  69.7 1.1 reshape.133
  70.9 9.6 %psum.7 = s32[8]{0:T(128)S(1)} all-reduce(s32[8]{0:T(128)S(1)} %reduce_sum.29), channel_id=1, replica_groups=mesh['rep'=8,'tp'=4] {'rep'}, use_global_device_ids=true, to_apply=%region_5.6 | all-reduce | flops 8 | bytes 64 | tf_op jit(solution)/shard_map/psum | solution.py:79
  80.5 0.1 copy.53
  80.6 0.1 div.59
  80.7 0.1 broadcast_in_dim.48
  80.9 288.3 %all-gather.6.cloned.1.call-done = bf16[2048,5120]{1,0:T(8,128)(2,1)} async-done(((bf16[2048,1280]{1,0:T(8,128)(2,1)}), bf16[2048,5120]{1,0:T(8,128)(2,1)}) %all-gather.6.cloned.1.call-update) | async-done | bytes 20971536 | tf_op jit(solution)/shard_map/all_gather | solution.py:87
  369.1 34.5 %fusion = bf16[5120,1280]{0,1:T(8,128)(2,1)} fusion(bf16[2048,5120]{1,0:T(8,128)(2,1)} %all-gather.6.cloned.1.call-done, bf16[2048,1280]{1,0:T(8,128)(2,1)} %param.14, f32[2048]{0:T(1024)S(1)} %div.60), kind=kOutput, calls=%fused_computation.1 | convolution fusion | flops 26857963520 | bytes 39329792 | tf_op jit(solution)/shard_map/dot_general | solution.py:89
  403.7 17.6 %copy.72 = bf16[5120,1280]{1,0:T(8,128)(2,1)} copy(bf16[5120,1280]{0,1:T(8,128)(2,1)} %fusion) | data formatting | bytes 26214400
  421.4 2.5 copy.94
  423.9 3.7 all-to-all-start
  427.6 4.9 copy.55
  432.5 5.1 copy.52
  437.5 4.8 copy.54
  442.3 72.5 %reduce-scatter.7.cloned.1.call-done = bf16[640,1280]{1,0:T(8,128)(2,1)} async-done(((bf16[5120,1280]{1,0:T(8,128)(2,1)}), bf16[640,1280]{1,0:T(8,128)(2,1)}) %reduce-scatter.7.cloned.1.call-update) | async-done | bytes 1638416
  514.8 2.8 copy.73
  517.6 6.7 %fusion.8 = f32[640,1280]{0,1:T(8,128)} fusion(bf16[640,1280]{0,1:T(8,128)(2,1)S(1)} %copy.73, f32[640,1280]{0,1:T(8,128)} %copy.54, f32[640,1280]{0,1:T(8,128)} %copy.52), kind=kLoop, calls=%fused_computation.12 | loop fusion | flops 9830400 | bytes 11468800 | tf_op jit(solution)/shard_map/div | solution.py:99
  524.4 7.5 %fusion.14 = f32[1024,1280]{1,0:T(8,128)} fusion(bf16[1024,640]{1,0:T(8,128)(2,1)S(1)} %bitcast.74, f32[640,1280]{0,1:T(8,128)} %copy.55, f32[640,1280]{0,1:T(8,128)} %fusion.8), kind=kOutput, calls=%fused_computation.23 | convolution fusion | flops 1680179200 | bytes 13107200 | tf_op jit(solution)/shard_map/dot_general | solution.py:133
  531.9 56.6 %reduce-scatter.5.cloned.1.call-done = f32[128,1280]{1,0:T(8,128)} async-done(((f32[1024,1280]{1,0:T(8,128)}), f32[128,1280]{1,0:T(8,128)}) %reduce-scatter.5.cloned.1.call-update) | async-done | bytes 655376 | tf_op jit(solution)/shard_map/reduce_scatter | solution.py:132
  588.5 1.8 convert_element_type.64
  590.4 4.7 copy.56
  595.1 28.0 %all-gather.8.cloned.1.call-done = bf16[128,5120]{1,0:T(8,128)(2,1)} async-done(((bf16[128,1280]{1,0:T(8,128)(2,1)}), bf16[128,5120]{1,0:T(8,128)(2,1)}) %all-gather.8.cloned.1.call-update) | async-done | bytes 1310736 | tf_op jit(solution)/shard_map/all_gather | solution.py:138
  623.1 2.5 copy.96
  (35 shorter events, 0.6 us)
Async XLA Ops:
  7.2 42.5 %copy-start = (bf16[4,32,5120]{2,1,0:T(8,128)(2,1)S(1)}, bf16[4,32,5120]{2,1,0:T(8,128)(2,1)}, u32[]{:S(2)}) copy-start(bf16[4,32,5120]{2,1,0:T(8,128)(2,1)} %param.19) | copy-start | bytes 3932164
  7.2 0.8 copy-start.7
  7.2 362.0 %all-gather.6.cloned.1.call-start = ((), (), s32[]{:S(2)}) async-start(), calls=%async_computation.4 | async-start | bytes 26214400 | tf_op jit(solution)/shard_map/all_gather | solution.py:87
  7.9 413.4 %all-gather.4.cloned.1.call-start = ((), (), s32[]{:S(2)}) async-start(), calls=%async_computation.3 | async-start | bytes 1638400 | tf_op jit(solution)/shard_map/all_gather | solution.py:130
  56.8 1.7 copy-start.5
  58.6 3.9 copy-start.2
  64.0 1.9 copy-start.4
  65.9 2.2 copy-start.3
  68.2 2.7 copy-start.6
  70.9 443.9 %reduce-scatter.7.cloned.1.call-start = ((), (), s32[]{:S(2)}) async-start(), calls=%async_computation.7 | async-start | bytes 14745600
  423.9 100.5 %all-to-all-start = ((bf16[128,8,640]{2,0,1:T(8,128)(2,1)}), bf16[128,8,640]{2,0,1:T(8,128)(2,1)S(1)}, u32[]{:S(2)}, u32[]{:S(2)}) async-start(bf16[128,8,640]{2,0,1:T(8,128)(2,1)} %bitcast.71), calls=%async_computation | async-start | bytes 2621440 | tf_op jit(solution)/shard_map/all_to_all | solution.py:131
  427.5 161.0 %reduce-scatter.5.cloned.1.call-start = ((), (), s32[]{:S(2)}) async-start(), calls=%async_computation.5 | async-start | bytes 5898240 | tf_op jit(solution)/shard_map/reduce_scatter | solution.py:132
  531.9 91.2 %all-gather.8.cloned.1.call-start = ((), (), s32[]{:S(2)}) async-start(), calls=%async_computation.6 | async-start | bytes 1638400 | tf_op jit(solution)/shard_map/all_gather | solution.py:138
  590.4 35.1 %copy-start.1 = (bf16[4,32,5120]{2,1,0:T(8,128)(2,1)S(1)}, bf16[4,32,5120]{2,1,0:T(8,128)(2,1)}, u32[]{:S(2)}) copy-start(bf16[4,32,5120]{2,1,0:T(8,128)(2,1)} %param.19) | copy-start | bytes 3932164
Sparse Core Ops, SparseCore 0:
  9.6 359.5 all-gather.5
  371.3 31.0 all-gather.3
  421.5 93.2 reduce-scatter.6
  532.0 56.5 reduce-scatter.4
  590.5 32.5 all-gather.7
where the time goes:
time: 634 us; the launch traced here: 632 us
  waiting for transfers between devices  446 us (70%)
  local copies, waits for them, and re-layouts  89.8 us (14%)
  matrix products  57.3 us (9%)
  between operations  14 us (2%)
  other arithmetic  11.4 us (2%)
  blocking collectives  9.6 us (2%)
    all_gather x1, waiting for transfers between devices, per_device(): features = lax.all_gather(context, 'tp', axis=1, tiled=True)  288 us
    unnamed x6, waiting for transfers between devices  73.3 us
    unnamed x24, local copies, waits for them, and re-layouts  61.9 us
    reduce_scatter x1, waiting for transfers between devices, per_device(): lax.psum_scatter(jnp.dot(feature_rows, weight, preferred_element_type=jnp...  56.6 us
    dot_general x1, matrix products, per_device(): lax.dot_general(features, scaled, (((0,), (0,)), ((), ())), preferred_ele...  34.5 us
    all_gather x1, waiting for transfers between devices, per_device(): lax.all_gather(own_columns.astype(jnp.bfloat16), 'tp', axis=1, tiled=True)  28 us
  transfers between devices with their start and end apart: 6, of which 4 were waited for; matrix products, arithmetic and copies ran while one was open for 23% of the time, Pallas kernels for 0%

commit v1 on v0

v1 whole, which is shorter than its diff:
```python
import math

import jax
import jax.numpy as jnp
from jax import lax
from jax.experimental.layout import Layout as MemoryLayout, with_layout_constraint
from jax.sharding import PartitionSpec as P


HEAD_DIM = 128


rope_base = 1000000.0
first_beta = 0.9
second_beta = 0.95
adam_epsilon = 1e-08
step_count = 10
learn_rate = 0.001


bf16 = jnp.bfloat16
f32 = jnp.float32
AXES = ("rep", "tp")
ROW_MAJOR = MemoryLayout(major_to_minor=(0, 1))


def rotate(vectors, positions):
    half_dim = vectors.shape[-1] // 2
    frequency = rope_base ** (-2.0 * jnp.arange(half_dim, dtype=jnp.float32) / vectors.shape[-1])
    angles = positions[..., None].astype(jnp.float32) * frequency
    cosine_table = jnp.cos(angles)
    sine_table = jnp.sin(angles)
    former = vectors[..., :half_dim]
    latter = vectors[..., half_dim:]
    return jnp.concatenate(
        [former * cosine_table - latter * sine_table, latter * cosine_table + former * sine_table],
        axis=-1,
    )


def attend(queries, old_keys, old_values, new_keys, new_values, live_mask):
    score_scale = HEAD_DIM ** (-0.5)
    step_total = queries.shape[0]
    cache_scores = (
        jnp.einsum("tsqd,scd->tsqc", queries, old_keys, preferred_element_type=jnp.float32)
        * score_scale
    )
    cache_scores = jnp.where(live_mask[None, :, None, :], cache_scores, -1e30)
    recent = (
        jnp.einsum("tsqd,usd->tsqu", queries, new_keys, preferred_element_type=jnp.float32)
        * score_scale
    )
    causal = jnp.arange(step_total)[:, None] >= jnp.arange(step_total)[None, :]
    recent = jnp.where(causal[:, None, None, :], recent, -1e30)
    row_peak = jnp.maximum(jnp.max(cache_scores, axis=-1), jnp.max(recent, axis=-1))[..., None]
    cache_exp = jnp.exp(cache_scores - row_peak)
    recent_exp = jnp.exp(recent - row_peak)
    denominator = jnp.sum(cache_exp, axis=-1, keepdims=True) + jnp.sum(
        recent_exp, axis=-1, keepdims=True
    )
    cache_weight = (cache_exp / denominator).astype(jnp.bfloat16)
    recent_weight = (recent_exp / denominator).astype(jnp.bfloat16)
    attended = jnp.einsum(
        "tsqc,scd->tsqd", cache_weight, old_values, preferred_element_type=jnp.float32
    )
    attended = attended + jnp.einsum(
        "tsqu,usd->tsqd", recent_weight, new_values, preferred_element_type=jnp.float32
    )
    return attended.astype(jnp.bfloat16)


def decode_heads(inputs, w_query, w_key, w_value, cache_keys, cache_values, lengths):
    step_total, seq_local, model_width = inputs.shape
    local_heads = w_query.shape[1] // HEAD_DIM
    local_kv = w_key.shape[1] // HEAD_DIM
    shared = local_heads // local_kv
    flat_rows = inputs.reshape(step_total * seq_local, model_width)
    query_flat = jnp.dot(flat_rows, w_query, preferred_element_type=jnp.float32)
    key_flat, value_flat = (
        jnp.dot(flat_rows, w, preferred_element_type=jnp.float32) for w in (w_key, w_value)
    )
    query_flat, key_flat, value_flat = lax.optimization_barrier(
        (query_flat, key_flat, value_flat)
    )
    seq_length = jnp.repeat(lengths, seq_local // lengths.shape[0])
    positions = seq_length[None, :] + jnp.arange(step_total, dtype=jnp.int32)[:, None]
    slot_total = cache_keys.shape[1]
    live_mask = jnp.arange(slot_total, dtype=jnp.int32)[None, :] < seq_length[:, None]
    heads = []
    for kv in range(local_kv):
        lanes = slice(kv * HEAD_DIM, (kv + 1) * HEAD_DIM)
        wide = slice(kv * shared * HEAD_DIM, (kv + 1) * shared * HEAD_DIM)
        queries = query_flat[:, wide].reshape(step_total, seq_local, shared, HEAD_DIM)
        queries = rotate(queries, positions[:, :, None]).astype(jnp.bfloat16)
        key_new = key_flat[:, lanes].reshape(step_total, seq_local, HEAD_DIM)
        key_new = rotate(key_new, positions).astype(jnp.bfloat16)
        value_new = value_flat[:, lanes].reshape(step_total, seq_local, HEAD_DIM)
        attended = attend(
            queries,
            cache_keys[:, :, lanes],
            cache_values[:, :, lanes],
            key_new,
            value_new.astype(jnp.bfloat16),
            live_mask,
        )
        heads.append(attended.reshape(step_total * seq_local, shared * HEAD_DIM))
    return jnp.concatenate(heads, axis=1)


def token_scale(rewards, totals, token_local):
    replicas = lax.axis_size("rep")
    prompt_count, local_group = rewards.shape
    group_size = local_group * replicas
    advantage = rewards.astype(jnp.float32) - totals.astype(jnp.float32)[:, None] / group_size
    return jnp.repeat(advantage.reshape(-1), token_local // (prompt_count * local_group)) / (
        token_local * replicas
    )


def adam(gradient, first_moment, second_moment):
    moment_new = first_beta * first_moment + (1.0 - first_beta) * gradient
    square_new = second_beta * second_moment + (1.0 - second_beta) * gradient * gradient
    return (
        moment_new
        / (1.0 - first_beta**step_count)
        / (jnp.sqrt(square_new / (1.0 - second_beta**step_count)) + adam_epsilon)
    )


def outer_sum(rows, columns):
    return lax.dot_general(
        rows, columns, (((0,), (0,)), ((), ())), preferred_element_type=jnp.float32
    )


def bits_below(count):
    found = []
    bit = 1
    while bit < count:
        found.append(bit)
        bit *= 2
    return found


def pick(array, index):
    return lax.dynamic_index_in_dim(array, index, 0, keepdims=False)


class Layout:
    def __init__(self, replicas, planes):
        self.replicas = replicas
        self.planes = planes
        self.split = replicas // planes
        self.group_bits = bits_below(planes)
        self.split_bits = bits_below(self.split)
        self.strides = range(1, planes // 2)

    def hub(self, pair):
        return 2 * pair + 1 if pair < self.planes // 4 or self.planes == 2 else 2 * pair

    def outer(self, pair):
        return self.hub(pair) ^ 1

    def is_hub(self, plane):
        return self.hub(plane // 2) == plane

    def far_hub(self, plane, stride):
        return self.hub((plane // 2) ^ stride)

    def crosses(self, stride):
        return bool(stride & (self.planes // 4))

    def table(self, values):
        return pick(jnp.array(values), lax.axis_index("tp"))

    def send(self, array, target):
        moves = []
        for rep in range(self.replicas):
            for plane in range(self.planes):
                to = target(rep // self.split, rep % self.split, plane)
                if to is not None:
                    group, part, other = to
                    moves.append(
                        (
                            rep * self.planes + plane,
                            (group * self.split + part) * self.planes + other,
                        )
                    )
        return lax.ppermute(array, AXES, moves)

    def group(self):
        return lax.axis_index("rep") // self.split

    def part(self):
        return lax.axis_index("rep") % self.split

    def sum_parts(self, blocks):
        part = self.part()
        for bit in reversed(self.split_bits):
            mine = (part // bit) % 2
            halves = [b.reshape((2, bit) + b.shape[1:]) for b in blocks]
            away = jnp.stack([pick(h, 1 - mine) for h in halves]).astype(bf16)
            got = self.send(away, lambda g, u, z, bit=bit: (g, u ^ bit, z))
            blocks = [pick(h, mine) + got[k].astype(f32) for k, h in enumerate(halves)]
        return [b[0] for b in blocks]

    def scatter_groups(self, pieces, index):
        half = pieces[0].shape[0] // 2
        live = [dict(enumerate(p[:half] for p in pieces))]
        live.append(dict(enumerate(p[half:] for p in pieces)))
        orders = [list(self.group_bits), list(reversed(self.group_bits))]
        for step in range(len(self.group_bits)):
            for c in range(2):
                bit = orders[c][step]
                mine = (index // bit) % 2 == 1
                low = [k for k in sorted(live[c]) if not k & bit]
                away = [jnp.where(mine, live[c][k], live[c][k | bit]).astype(bf16) for k in low]
                got = self.send(
                    jnp.concatenate(away, axis=0), lambda g, u, z, bit=bit: (g ^ bit, u, z)
                )
                got = jnp.split(got, len(low), axis=0)
                live[c] = {
                    k: jnp.where(mine, live[c][k | bit], live[c][k]) + got[n].astype(f32)
                    for n, k in enumerate(low)
                }
        return jnp.concatenate([live[0][0], live[1][0]], axis=0)

    def gather_planes(self, block):
        plane = lax.axis_index("tp")
        found = [(plane, block)]
        partner = self.send(block, lambda g, u, z: (g, u, z ^ 1))
        hub_here = self.table([self.is_hub(z) for z in range(self.planes)])

        def out(g, u, z):
            return (g, u, z ^ 1) if self.is_hub(z) else None

        for name, source in (("hub", block), ("outer", partner)):
            for stride in self.strides:

                def hop(g, u, z, stride=stride):
                    return (g, u, self.far_hub(z, stride)) if self.is_hub(z) else None

                got = self.send(source, hop)
                passed = self.send(got, out)
                order = [self.far_hub(z, stride) for z in range(self.planes)]
                if name == "outer":
                    order = [z ^ 1 for z in order]
                found.append((self.table(order), jnp.where(hub_here, got, passed)))
            if name == "hub":
                found.insert(1, (plane ^ 1, partner))
        return found


DECODE_CHUNKS = 2


def chunk_widths(rows):
    unit = math.gcd(rows, 128)
    units = rows // unit
    if units < 3:
        return [unit] * units
    rest = units - 1
    return [unit * (rest - rest // 2), unit * (rest // 2), unit]


def per_device(
    context,
    out_grad,
    rewards,
    master,
    first_moment,
    second_moment,
    inputs,
    w_query,
    w_key,
    w_value,
    cache_keys,
    cache_values,
    lengths,
):
    replicas = lax.axis_size("rep")
    planes = lax.axis_size("tp")
    lay = Layout(replicas, planes)
    split = lay.split
    tokens, features = context.shape
    columns = out_grad.shape[1]
    own_rows = features // split
    plane = lax.axis_index("tp")

    pair_grad = lay.send(out_grad, lambda g, u, z: (g, u, z ^ 1))
    crossing = [s for s in lay.strides if lay.crosses(s)]
    hub_rows = {
        s: lay.send(
            context,
            lambda g, u, z, s=s: (g, u, lay.far_hub(z, s)) if lay.is_hub(z) else None,
        )
        for s in crossing
    }
    widths = chunk_widths(own_rows)
    spots = [slice(sum(widths[:k]), sum(widths[: k + 1])) for k in range(len(widths))]

    def chunk_of(rows, spot):
        return jnp.concatenate(
            [rows[:, u * own_rows + spot.start : u * own_rows + spot.stop] for u in range(split)],
            axis=1,
        )

    chunks = [chunk_of(context, spot) for spot in spots]

    def send_far(chunk):
        found = {}
        for s in lay.strides:
            if lay.crosses(s):
                found[s] = lay.send(
                    chunk,
                    lambda g, u, z, s=s: None if lay.is_hub(z) else (g, u, lay.far_hub(z, s)),
                )
            else:
                found[s] = lay.send(chunk, lambda g, u, z, s=s: (g, u, z ^ (2 * s)))
        return found

    totals = lax.psum(jnp.sum(rewards, axis=1), "rep")
    inputs, totals = lax.optimization_barrier((inputs, totals))
    scale = token_scale(rewards, totals, tokens)[:, None]
    own_grad = lax.optimization_barrier((out_grad.astype(f32) * scale).astype(bf16))

    attended = decode_heads(inputs, w_query, w_key, w_value, cache_keys, cache_values, lengths)
    pieces = lay.gather_planes(attended)
    partner, *chunks = lax.optimization_barrier((pieces[1][1], *chunks))
    pieces[1] = (pieces[1][0], partner)
    all_heads = jnp.zeros((attended.shape[0], features * planes), bf16)
    for index, piece in pieces:
        all_heads = lax.dynamic_update_slice_in_dim(all_heads, piece, index * features, 1)
    far_rows = []
    for k, chunk in enumerate(chunks):
        if k > 1:
            names = list(far_rows[k - 2])
            chunk, *before = lax.optimization_barrier((chunk, *far_rows[k - 2].values()))
            far_rows[k - 2] = dict(zip(names, before))
        far_rows.append(send_far(chunk))
    feature_rows = lax.all_to_all(all_heads, "rep", split_axis=1, concat_axis=0, tiled=True)
    feature_rows = with_layout_constraint(feature_rows, ROW_MAJOR)

    def product(rows, grads):
        return outer_sum(rows, grads).reshape(split, rows.shape[1] // split, columns)

    own_own = product(context, own_grad)
    own_own, pair_grad = lax.optimization_barrier((own_own, pair_grad))
    pair_grad = lax.optimization_barrier((pair_grad.astype(f32) * scale).astype(bf16))
    hub_here = lay.table([lay.is_hub(z) for z in range(planes)])
    passed = []
    for k, spot in enumerate(spots):
        onward = {s: chunk_of(hub_rows[s], spot) for s in crossing}
        if k > 1 and crossing:
            tied = lax.optimization_barrier((onward, passed[k - 2]))
            onward, passed[k - 2] = tied
        passed.append(
            {
                s: lay.send(
                    onward[s], lambda g, u, z: (g, u, z ^ 1) if lay.is_hub(z) else None
                )
                for s in crossing
            }
        )
    own_other = product(context, pair_grad)
    own_sums = lay.sum_parts([own_own, own_other])

    relative = lay.group() ^ plane
    odd = relative % 2 == 1

    def swap(g, u, z):
        return (g ^ 1, u, z ^ 1) if (g ^ z) & 1 else None

    steps = []
    weights = []
    for k, spot in enumerate(spots):
        parts = []
        for s in lay.strides:
            rows = far_rows[k][s]
            if s in passed[k]:
                rows = lax.optimization_barrier(jnp.where(hub_here, rows, passed[k][s]))
            parts += [product(rows, own_grad), product(rows, pair_grad)]
        sums = [block[spot] for block in own_sums]
        if parts:
            sums += lay.sum_parts(parts)
        kept = lay.scatter_groups(sums, relative).astype(bf16)
        gradient = jnp.where(odd, lay.send(kept, swap), kept)
        step = adam(gradient.astype(f32), first_moment[spot], second_moment[spot])
        steps.append(step)
        weights.append((master[spot] - learn_rate * step).astype(bf16))

    step_total, seq_local, model_width = inputs.shape
    local_tokens = step_total * seq_local
    decoded = jnp.zeros((local_tokens, model_width), bf16)
    strip = columns // DECODE_CHUNKS
    for d in range(DECODE_CHUNKS):
        cols = slice(d * strip, (d + 1) * strip)
        partial = 0.0
        if len(weights) > 1:
            head = jnp.concatenate([w[:, cols] for w in weights[:-1]], axis=0)
            partial = jnp.dot(
                feature_rows[:, : spots[-1].start], head, preferred_element_type=f32
            )
            partial = lax.optimization_barrier(partial)
        partial = partial + jnp.dot(
            feature_rows[:, spots[-1]], weights[-1][:, cols], preferred_element_type=f32
        )
        partial = with_layout_constraint(partial, ROW_MAJOR)
        by_part = partial.reshape(planes, split, local_tokens, strip)
        by_part = lay.sum_parts([jnp.moveaxis(by_part, 1, 0)])[0]
        own = lay.scatter_groups([by_part[g] for g in range(planes)], lay.group()).astype(bf16)
        if d == DECODE_CHUNKS - 1:
            own, *steps = lax.optimization_barrier((own, *steps))
        for index, piece in lay.gather_planes(own):
            decoded = lax.dynamic_update_slice(
                decoded, piece, (0, index * columns + d * strip)
            )
    adam_step = jnp.concatenate(steps, axis=0)
    return (decoded.reshape(step_total, seq_local, model_width), adam_step)


def solution(mesh):
    placed = (
        P("rep", "tp"),
        P("rep", "tp"),
        P(None, "rep"),
        P("rep", "tp"),
        P("rep", "tp"),
        P("rep", "tp"),
        P(None, "rep", None),
        P(None, "tp"),
        P(None, "tp"),
        P(None, "tp"),
        P("rep", None, "tp"),
        P("rep", None, "tp"),
        P("rep"),
    )

    return jax.shard_map(
        per_device,
        mesh=mesh,
        in_specs=placed,
        out_specs=(P(None, "rep", None), P("rep", "tp")),
        check_vma=False,
    )
```

time: 634 us -> 615 us (0.970); the launches traced: 632 us -> 606 us
  waiting for transfers between devices: 446 us -> 342 us
  starting transfers between devices: 3.87 us -> 86.2 us
  other arithmetic: 11.4 us -> 60 us
  local copies, waits for them, and re-layouts: 89.8 us -> 43.8 us
  between operations: 14 us -> 3.51 us
    ppermute x0 -> x52, waiting for transfers between devices: none -> 342 us  [send(): return lax.ppermute(array, AXES, moves)]
    all_gather x3 -> x0, waiting for transfers between devices: 316 us -> none  [the longest x1 288 us: per_device(): features = lax.all_gather(context, 'tp', axis=1, tiled=True)]
    ppermute x0 -> x52, starting transfers between devices: none -> 82 us  [send(): return lax.ppermute(array, AXES, moves)]
    unnamed x6 -> x0, waiting for transfers between devices: 73.3 us -> none
    reduce_scatter x1 -> x0, waiting for transfers between devices: 56.6 us -> none  [per_device(): lax.psum_scatter(jnp.dot(feature_rows, weight, preferred_element_type=jnp...]
    unnamed x24 -> x83, local copies, waits for them, and re-layouts: 61.9 us -> 8.75 us
    convert_element_type x1 -> x13, other arithmetic: 1.84 us -> 17.7 us  [the longest x2 8.12 us: per_device(): weights.append((master[spot] - learn_rate * step).astype(bf16))]
    reshape x3 -> x2, local copies, waits for them, and re-layouts: 15.6 us -> 0.1 us  [decode_heads(): query_flat[:, wide].reshape(step_total, seq_local, shared, HEAD_DIM)]
  transfers between devices with their start and end apart: 6 -> 53, of which waited for: 4 -> 17; matrix products, arithmetic and copies ran while one was open for 23% -> 21% of each run, Pallas kernels for 0% -> 0%
where the time goes in v1:
time: 615 us; the launch traced here: 606 us
  waiting for transfers between devices  342 us (56%)
  starting transfers between devices  86.2 us (14%)
  matrix products  61.6 us (10%)
  other arithmetic  60 us (10%)
  local copies, waits for them, and re-layouts  43.8 us (7%)
  blocking collectives  9.5 us (2%)
    ppermute x52, waiting for transfers between devices, send(): return lax.ppermute(array, AXES, moves)  342 us
    ppermute x52, starting transfers between devices, send(): return lax.ppermute(array, AXES, moves)  82 us
    dot_general x8, matrix products, outer_sum(): lax.dot_general(rows, columns, (((0,), (0,)), ((), ())), preferred_elemen...  39.6 us
  transfers between devices with their start and end apart: 53, of which 17 were waited for; matrix products, arithmetic and copies ran while one was open for 21% of the time, Pallas kernels for 0%

profile of v1, /device:TPU:0, one launch (start us, length us, event | category | flops | bytes accessed | tf_op | source)
XLA Modules:
  0.0 606.4 jit_solution(15241603343799166026)
XLA Ops:
  2.5 9.5 %psum.7 = s32[8]{0:T(128)S(1)} all-reduce(s32[8]{0:T(128)S(1)} %reduce_sum.45), channel_id=1, replica_groups=mesh['rep'=8,'tp'=4] {'rep'}, use_global_device_ids=true, to_apply=%region_1.0 | all-reduce | flops 8 | bytes 64 | tf_op jit(solution)/shard_map/psum | solution.py:322
  12.0 2.0 fusion.162
  15.0 6.6 %fusion.160 = f32[128,1280]{1,0:T(8,128)S(1)} fusion(bf16[128,5120]{1,0:T(8,128)(2,1)S(1)} %bitcast.368, bf16[5120,1280]{1,0:T(8,128)(2,1)} %param.30), kind=kOutput, calls=%fused_computation.312 | convolution fusion | flops 1677721600 | bytes 15073280 | tf_op jit(solution)/shard_map/dot_general | solution.py:78
  33.4 4.4 collective-permute-start
  37.9 3.1 collective-permute-start.6
  41.3 3.4 multiply_convert_fusion.1
  44.7 2.2 fusion.145
  46.9 2.5 fusion.146
  49.4 2.4 pad_maximum_fusion.2
  52.9 4.4 collective-permute-start.5
  57.3 11.0 %fusion.163 = f32[1280,1280]{0,1:T(8,128)} fusion(bf16[2048,1280]{1,0:T(8,128)(2,1)S(1)} %multiply_convert_fusion.1, bf16[2048,1280]{1,0:T(8,128)(2,1)} %param.23), kind=kOutput, calls=%fused_computation.315 | convolution fusion | flops 6710886400 | bytes 17039360 | tf_op jit(solution)/shard_map/dot_general | solution.py:131
  78.5 84.6 %collective-permute-done.2 = bf16[128,1280]{1,0:T(8,128)(2,1)S(1)} collective-permute-done((bf16[128,1280]{1,0:T(8,128)(2,1)S(1)}, bf16[128,1280]{1,0:T(8,128)(2,1)S(1)}, u32[]{:S(2)}, u32[]{:S(2)}) %collective-permute-start.2) | collective-permute-done | bytes 327712 | tf_op jit(solution)/shard_map/ppermute | solution.py:189
  163.1 2.6 collective-permute-start.16
  168.6 92.3 %collective-permute-done.4 = bf16[128,1280]{1,0:T(8,128)(2,1)} collective-permute-done((bf16[128,1280]{1,0:T(8,128)(2,1)}, bf16[128,1280]{1,0:T(8,128)(2,1)}, u32[]{:S(2)}, u32[]{:S(2)}) %collective-permute-start.4) | collective-permute-done | bytes 327712 | tf_op jit(solution)/shard_map/ppermute | solution.py:189
  263.5 4.3 all-to-all-start
  267.8 2.9 collective-permute-start.24
  270.7 2.5 fusion.143
  278.7 3.5 multiply_convert_fusion
  282.3 10.0 %fusion.166 = f32[1280,1280]{0,1:T(8,128)S(1)} fusion(bf16[2048,1280]{1,0:T(8,128)(2,1)S(1)} %multiply_convert_fusion, bf16[2048,1280]{1,0:T(8,128)(2,1)} %param.23), kind=kOutput, calls=%fused_computation.318 | convolution fusion | flops 6710886400 | bytes 17039360 | tf_op jit(solution)/shard_map/dot_general | solution.py:131
  294.7 30.7 %collective-permute-done.17 = bf16[2048,512]{1,0:T(8,128)(2,1)} collective-permute-done((bf16[2048,512]{1,0:T(8,128)(2,1)}, bf16[2048,512]{1,0:T(8,128)(2,1)}, u32[]{:S(2)}, u32[]{:S(2)}) %collective-permute-start.17) | collective-permute-done | bytes 2097184 | tf_op jit(solution)/shard_map/ppermute | solution.py:189
  325.4 2.4 broadcast_select_fusion
  327.9 4.4 fusion.168
  332.3 4.5 fusion.167
  336.8 32.5 %collective-permute-done.7 = bf16[2048,512]{1,0:T(8,128)(2,1)S(1)} collective-permute-done((bf16[2048,512]{1,0:T(8,128)(2,1)}, bf16[2048,512]{1,0:T(8,128)(2,1)S(1)}, u32[]{:S(2)}, u32[]{:S(2)}) %collective-permute-start.7) | collective-permute-done | bytes 2097184 | tf_op jit(solution)/shard_map/ppermute | solution.py:189
  370.2 3.0 fusion.165
  373.3 3.4 fusion.164
  383.9 19.1 %collective-permute-done.25 = bf16[2048,256]{1,0:T(8,128)(2,1)S(1)} collective-permute-done((bf16[2048,256]{1,0:T(8,128)(2,1)S(1)}, bf16[2048,256]{1,0:T(8,128)(2,1)S(1)}, u32[]{:S(2)}, u32[]{:S(2)}) %collective-permute-start.25) | collective-permute-done | bytes 1048608 | tf_op jit(solution)/shard_map/ppermute | solution.py:189
  409.1 1.9 convert_add_fusion
  412.1 2.1 add_bitcast_fusion.1
  422.7 25.5 %collective-permute-done.21 = bf16[256,1280]{1,0:T(8,128)(2,1)S(1)} collective-permute-done((bf16[256,1280]{1,0:T(8,128)(2,1)S(1)}, bf16[256,1280]{1,0:T(8,128)(2,1)S(1)}, u32[]{:S(2)}, u32[]{:S(2)}) %collective-permute-start.21) | collective-permute-done | bytes 655392 | tf_op jit(solution)/shard_map/ppermute | solution.py:189
  451.6 5.3 collective-permute-done.27
  460.8 4.9 collective-permute-done.28
  470.4 1.9 collective-permute-done.12
  476.5 23.0 %collective-permute-done.14 = bf16[128,1280]{1,0:T(8,128)(2,1)S(1)} collective-permute-done((bf16[128,1280]{1,0:T(8,128)(2,1)S(1)}, bf16[128,1280]{1,0:T(8,128)(2,1)S(1)}, u32[]{:S(2)}, u32[]{:S(2)}) %collective-permute-start.14) | collective-permute-done | bytes 327712 | tf_op jit(solution)/shard_map/ppermute | solution.py:189
  502.3 1.9 copy.104
  504.2 3.0 subtract_convert_fusion.2
  507.2 5.1 subtract_convert_fusion.1
  516.6 2.5 fusion.63
  520.7 2.2 convolution_add_fusion.1
  531.8 16.0 %collective-permute-start.33 = (bf16[128,640]{0,1:T(8,128)(2,1)S(1)}, bf16[128,640]{0,1:T(8,128)(2,1)S(1)}, u32[]{:S(2)}, u32[]{:S(2)}) collective-permute-start(bf16[128,640]{0,1:T(8,128)(2,1)S(1)} %pad_maximum_fusion.22), channel_id=1, source_target_pairs={{0,8},{1,9},{2,10},{3,11},{4,12},{5,13},{6,14},{7,15},{8,0},{9,1},... | collective-permute-start | bytes 491528 | tf_op jit(solution)/shard_map/ppermute | solution.py:189
  548.7 4.1 collective-permute-done.33
  553.6 1.8 collective-permute-done.43
  559.3 2.6 collective-permute-start.36
  564.2 1.8 collective-permute-start.47
  575.8 3.2 pad_maximum_fusion.1
  583.6 4.9 collective-permute-done.39
  589.8 7.6 %collective-permute-done.41 = bf16[128,640]{0,1:T(8,128)(2,1)S(1)} collective-permute-done((bf16[128,640]{0,1:T(8,128)(2,1)S(1)}, bf16[128,640]{0,1:T(8,128)(2,1)S(1)}, u32[]{:S(2)}, u32[]{:S(2)}) %collective-permute-start.41) | collective-permute-done | bytes 163872 | tf_op jit(solution)/shard_map/ppermute | solution.py:189
  603.8 2.4 copy.124
  (300 shorter events, 125.0 us)
Async XLA Ops:
  32.7 37.3 %collective-permute-start.1 = (bf16[128,1280]{1,0:T(8,128)(2,1)S(1)}, bf16[128,1280]{1,0:T(8,128)(2,1)S(1)}, u32[]{:S(2)}, u32[]{:S(2)}) collective-permute-start(bf16[128,1280]{1,0:T(8,128)(2,1)S(1)} %bitcast_dynamic-update-slice_fusion), channel_id=1, source_target_pairs={{1,2},{2,1},{5,6},{6,5},{9,10},{10,9},{13,14},{14,13},{17,18},{18,... | collective-permute-start | bytes 983048 | tf_op jit(solution)/shard_map/ppermute | solution.py:189
  33.4 19.5 %collective-permute-start = (bf16[128,1280]{1,0:T(8,128)(2,1)S(1)}, bf16[128,1280]{1,0:T(8,128)(2,1)}, u32[]{:S(2)}, u32[]{:S(2)}) collective-permute-start(bf16[128,1280]{1,0:T(8,128)(2,1)S(1)} %bitcast_dynamic-update-slice_fusion), channel_id=1, source_target_pairs={{0,1},{1,0},{2,3},{3,2},{4,5},{5,4},{6,7},{7,6},{8,9},{9,8},{10,11... | collective-permute-start | bytes 983048 | tf_op jit(solution)/shard_map/ppermute | solution.py:189
  37.8 240.9 %collective-permute-start.8 = (bf16[2048,1280]{1,0:T(8,128)(2,1)}, bf16[2048,1280]{1,0:T(8,128)(2,1)}, u32[]{:S(2)}, u32[]{:S(2)}) collective-permute-start(bf16[2048,1280]{1,0:T(8,128)(2,1)} %param.24), channel_id=1, source_target_pairs={{0,1},{1,0},{2,3},{3,2},{4,5},{5,4},{6,7},{7,6},{8,9},{9,8},{10,11... | collective-permute-start | bytes 15728648 | tf_op jit(solution)/shard_map/ppermute | solution.py:189
  37.9 232.8 %collective-permute-start.6 = (bf16[2048,1280]{1,0:T(8,128)(2,1)}, bf16[2048,1280]{1,0:T(8,128)(2,1)}, u32[]{:S(2)}, u32[]{:S(2)}) collective-permute-start(bf16[2048,1280]{1,0:T(8,128)(2,1)} %param.23), channel_id=1, source_target_pairs={{1,2},{2,1},{5,6},{6,5},{9,10},{10,9},{13,14},{14,13},{17,18},{18,... | collective-permute-start | bytes 15728648 | tf_op jit(solution)/shard_map/ppermute | solution.py:189
  52.9 214.9 %collective-permute-start.5 = (bf16[2048,512]{1,0:T(8,128)(2,1)}, bf16[2048,512]{1,0:T(8,128)(2,1)S(1)}, u32[]{:S(2)}, u32[]{:S(2)}) collective-permute-start(bf16[2048,512]{1,0:T(8,128)(2,1)} %get-tuple-element.27), channel_id=1, source_target_pairs={{0,2},{3,1},{4,6},{7,5},{8,10},{11,9},{12,14},{15,13},{16,18},{19,... | collective-permute-start | bytes 6291464 | tf_op jit(solution)/shard_map/ppermute | solution.py:189
  68.6 97.1 %collective-permute-start.3 = (bf16[128,1280]{1,0:T(8,128)(2,1)}, bf16[128,1280]{1,0:T(8,128)(2,1)}, u32[]{:S(2)}, u32[]{:S(2)}) collective-permute-start(bf16[128,1280]{1,0:T(8,128)(2,1)} %collective-permute-done), channel_id=1, source_target_pairs={{1,2},{2,1},{5,6},{6,5},{9,10},{10,9},{13,14},{14,13},{17,18},{18,... | collective-permute-start | bytes 983048 | tf_op jit(solution)/shard_map/ppermute | solution.py:189
  70.0 93.1 %collective-permute-start.2 = (bf16[128,1280]{1,0:T(8,128)(2,1)S(1)}, bf16[128,1280]{1,0:T(8,128)(2,1)S(1)}, u32[]{:S(2)}, u32[]{:S(2)}) collective-permute-start(bf16[128,1280]{1,0:T(8,128)(2,1)S(1)} %collective-permute-done.1), channel_id=1, source_target_pairs={{1,0},{2,3},{5,4},{6,7},{9,8},{10,11},{13,12},{14,15},{17,16},{18,... | collective-permute-start | bytes 983048 | tf_op jit(solution)/shard_map/ppermute | solution.py:189
  163.1 131.6 %collective-permute-start.16 = (bf16[2048,512]{1,0:T(8,128)(2,1)}, bf16[2048,512]{1,0:T(8,128)(2,1)}, u32[]{:S(2)}, u32[]{:S(2)}) collective-permute-start(bf16[2048,512]{1,0:T(8,128)(2,1)} %get-tuple-element.33), channel_id=1, source_target_pairs={{0,2},{3,1},{4,6},{7,5},{8,10},{11,9},{12,14},{15,13},{16,18},{19,... | collective-permute-start | bytes 6291464 | tf_op jit(solution)/shard_map/ppermute | solution.py:189
  165.7 95.2 %collective-permute-start.4 = (bf16[128,1280]{1,0:T(8,128)(2,1)}, bf16[128,1280]{1,0:T(8,128)(2,1)}, u32[]{:S(2)}, u32[]{:S(2)}) collective-permute-start(bf16[128,1280]{1,0:T(8,128)(2,1)} %collective-permute-done.3), channel_id=1, source_target_pairs={{1,0},{2,3},{5,4},{6,7},{9,8},{10,11},{13,12},{14,15},{17,16},{18,... | collective-permute-start | bytes 983048 | tf_op jit(solution)/shard_map/ppermute | solution.py:189
  263.5 238.8 %all-to-all-start = ((bf16[128,8,640]{0,2,1:T(8,128)(2,1)}), bf16[128,8,640]{0,2,1:T(8,128)(2,1)}, u32[]{:S(2)}, u32[]{:S(2)}) async-start(bf16[128,8,640]{0,2,1:T(8,128)(2,1)} %bitcast.30), calls=%async_computation | async-start | bytes 2621440 | tf_op jit(solution)/shard_map/all_to_all | solution.py:341
  267.8 116.1 %collective-permute-start.24 = (bf16[2048,256]{1,0:T(8,128)(2,1)}, bf16[2048,256]{1,0:T(8,128)(2,1)}, u32[]{:S(2)}, u32[]{:S(2)}) collective-permute-start(bf16[2048,256]{1,0:T(8,128)(2,1)} %pad_maximum_fusion.8), channel_id=1, source_target_pairs={{0,2},{3,1},{4,6},{7,5},{8,10},{11,9},{12,14},{15,13},{16,18},{19,... | collective-permute-start | bytes 3145736 | tf_op jit(solution)/shard_map/ppermute | solution.py:189
  274.7 50.7 %collective-permute-start.17 = (bf16[2048,512]{1,0:T(8,128)(2,1)}, bf16[2048,512]{1,0:T(8,128)(2,1)}, u32[]{:S(2)}, u32[]{:S(2)}) collective-permute-start(bf16[2048,512]{1,0:T(8,128)(2,1)} %pad_maximum_fusion.5), channel_id=1, source_target_pairs={{1,0},{2,3},{5,4},{6,7},{9,8},{10,11},{13,12},{14,15},{17,16},{18,... | collective-permute-start | bytes 6291464 | tf_op jit(solution)/shard_map/ppermute | solution.py:189
  277.4 91.9 %collective-permute-start.7 = (bf16[2048,512]{1,0:T(8,128)(2,1)}, bf16[2048,512]{1,0:T(8,128)(2,1)S(1)}, u32[]{:S(2)}, u32[]{:S(2)}) collective-permute-start(bf16[2048,512]{1,0:T(8,128)(2,1)} %pad_maximum_fusion.4), channel_id=1, source_target_pairs={{1,0},{2,3},{5,4},{6,7},{9,8},{10,11},{13,12},{14,15},{17,16},{18,... | collective-permute-start | bytes 6291464 | tf_op jit(solution)/shard_map/ppermute | solution.py:189
  293.0 114.1 %collective-permute-start.10 = (bf16[2,1,640,1280]{3,2,1,0:T(8,128)(2,1)S(1)}, bf16[2,1,640,1280]{3,2,1,0:T(8,128)(2,1)S(1)}, u32[]{:S(2)}, u32[]{:S(2)}) collective-permute-start(bf16[2,1,640,1280]{3,2,1,0:T(8,128)(2,1)S(1)} %pad_maximum_fusion), channel_id=1, source_target_pairs={{0,4},{1,5},{2,6},{3,7},{4,0},{5,1},{6,2},{7,3},{8,12},{9,13},{10,... | collective-permute-start | bytes 9830408 | tf_op jit(solution)/shard_map/ppermute | solution.py:189
  376.7 26.2 %collective-permute-start.25 = (bf16[2048,256]{1,0:T(8,128)(2,1)S(1)}, bf16[2048,256]{1,0:T(8,128)(2,1)S(1)}, u32[]{:S(2)}, u32[]{:S(2)}) collective-permute-start(bf16[2048,256]{1,0:T(8,128)(2,1)S(1)} %pad_maximum_fusion.9), channel_id=1, source_target_pairs={{1,0},{2,3},{5,4},{6,7},{9,8},{10,11},{13,12},{14,15},{17,16},{18,... | collective-permute-start | bytes 3145736 | tf_op jit(solution)/shard_map/ppermute | solution.py:189
  382.0 29.1 %collective-permute-start.18 = (bf16[2,1,256,1280]{3,2,1,0:T(8,128)(2,1)}, bf16[2,1,256,1280]{3,2,1,0:T(8,128)(2,1)}, u32[]{:S(2)}, u32[]{:S(2)}) collective-permute-start(bf16[2,1,256,1280]{3,2,1,0:T(8,128)(2,1)} %pad_maximum_fusion.7), channel_id=1, source_target_pairs={{0,4},{1,5},{2,6},{3,7},{4,0},{5,1},{6,2},{7,3},{8,12},{9,13},{10,... | collective-permute-start | bytes 3932168 | tf_op jit(solution)/shard_map/ppermute | solution.py:189
  383.4 30.8 %collective-permute-start.9 = (bf16[2,1,256,1280]{3,2,1,0:T(8,128)(2,1)}, bf16[2,1,256,1280]{3,2,1,0:T(8,128)(2,1)}, u32[]{:S(2)}, u32[]{:S(2)}) collective-permute-start(bf16[2,1,256,1280]{3,2,1,0:T(8,128)(2,1)} %pad_maximum_fusion.6), channel_id=1, source_target_pairs={{0,4},{1,5},{2,6},{3,7},{4,0},{5,1},{6,2},{7,3},{8,12},{9,13},{10,... | collective-permute-start | bytes 3932168 | tf_op jit(solution)/shard_map/ppermute | solution.py:189
  407.0 13.9 %collective-permute-start.26 = (bf16[2,1,128,1280]{3,2,1,0:T(8,128)(2,1)S(1)}, bf16[2,1,128,1280]{3,2,1,0:T(8,128)(2,1)S(1)}, u32[]{:S(2)}, u32[]{:S(2)}) collective-permute-start(bf16[2,1,128,1280]{3,2,1,0:T(8,128)(2,1)S(1)} %pad_maximum_fusion.16), channel_id=1, source_target_pairs={{0,4},{1,5},{2,6},{3,7},{4,0},{5,1},{6,2},{7,3},{8,12},{9,13},{10,... | collective-permute-start | bytes 1966088 | tf_op jit(solution)/shard_map/ppermute | solution.py:189
  416.4 53.9 %collective-permute-start.13 = (bf16[256,1280]{1,0:T(8,128)(2,1)S(1)}, bf16[256,1280]{1,0:T(8,128)(2,1)S(1)}, u32[]{:S(2)}, u32[]{:S(2)}) collective-permute-start(bf16[256,1280]{1,0:T(8,128)(2,1)S(1)} %pad_maximum_fusion.11), channel_id=1, source_target_pairs={{0,16},{1,17},{2,18},{3,19},{4,20},{5,21},{6,22},{7,23},{8,24},{9,... | collective-permute-start | bytes 1966088 | tf_op jit(solution)/shard_map/ppermute | solution.py:189
  418.0 30.2 %collective-permute-start.21 = (bf16[256,1280]{1,0:T(8,128)(2,1)S(1)}, bf16[256,1280]{1,0:T(8,128)(2,1)S(1)}, u32[]{:S(2)}, u32[]{:S(2)}) collective-permute-start(bf16[256,1280]{1,0:T(8,128)(2,1)S(1)} %pad_maximum_fusion.14), channel_id=1, source_target_pairs={{0,16},{1,17},{2,18},{3,19},{4,20},{5,21},{6,22},{7,23},{8,24},{9,... | collective-permute-start | bytes 1966088 | tf_op jit(solution)/shard_map/ppermute | solution.py:189
  418.7 30.9 %collective-permute-start.19 = (bf16[256,1280]{1,0:T(8,128)(2,1)S(1)}, bf16[256,1280]{1,0:T(8,128)(2,1)S(1)}, u32[]{:S(2)}, u32[]{:S(2)}) collective-permute-start(bf16[256,1280]{1,0:T(8,128)(2,1)S(1)} %pad_maximum_fusion.13), channel_id=1, source_target_pairs={{0,8},{1,9},{2,10},{3,11},{4,12},{5,13},{6,14},{7,15},{8,0},{9,1},... | collective-permute-start | bytes 1966088 | tf_op jit(solution)/shard_map/ppermute | solution.py:189
  420.2 38.2 %collective-permute-start.11 = (bf16[256,1280]{1,0:T(8,128)(2,1)S(1)}, bf16[256,1280]{1,0:T(8,128)(2,1)S(1)}, u32[]{:S(2)}, u32[]{:S(2)}) collective-permute-start(bf16[256,1280]{1,0:T(8,128)(2,1)S(1)} %pad_maximum_fusion.10), channel_id=1, source_target_pairs={{0,8},{1,9},{2,10},{3,11},{4,12},{5,13},{6,14},{7,15},{8,0},{9,1},... | collective-permute-start | bytes 1966088 | tf_op jit(solution)/shard_map/ppermute | solution.py:189
  421.2 39.0 %collective-permute-start.29 = (bf16[128,1280]{1,0:T(8,128)(2,1)S(1)}, bf16[128,1280]{1,0:T(8,128)(2,1)S(1)}, u32[]{:S(2)}, u32[]{:S(2)}) collective-permute-start(bf16[128,1280]{1,0:T(8,128)(2,1)S(1)} %pad_maximum_fusion.18), channel_id=1, source_target_pairs={{0,16},{1,17},{2,18},{3,19},{4,20},{5,21},{6,22},{7,23},{8,24},{9,... | collective-permute-start | bytes 983048 | tf_op jit(solution)/shard_map/ppermute | solution.py:189
  448.1 8.8 %collective-permute-start.27 = (bf16[128,1280]{1,0:T(8,128)(2,1)S(1)}, bf16[128,1280]{1,0:T(8,128)(2,1)S(1)}, u32[]{:S(2)}, u32[]{:S(2)}) collective-permute-start(bf16[128,1280]{1,0:T(8,128)(2,1)S(1)} %pad_maximum_fusion.17), channel_id=1, source_target_pairs={{0,8},{1,9},{2,10},{3,11},{4,12},{5,13},{6,14},{7,15},{8,0},{9,1},... | collective-permute-start | bytes 983048 | tf_op jit(solution)/shard_map/ppermute | solution.py:189
  450.0 17.4 %collective-permute-start.20 = (bf16[128,1280]{1,0:T(8,128)(2,1)S(1)}, bf16[128,1280]{1,0:T(8,128)(2,1)S(1)}, u32[]{:S(2)}, u32[]{:S(2)}) collective-permute-start(bf16[128,1280]{1,0:T(8,128)(2,1)S(1)} %get-tuple-element.56), channel_id=1, source_target_pairs={{0,16},{1,17},{2,18},{3,19},{4,20},{5,21},{6,22},{7,23},{8,24},{9,... | collective-permute-start | bytes 983048 | tf_op jit(solution)/shard_map/ppermute | solution.py:189
  456.9 10.5 %collective-permute-start.22 = (bf16[128,1280]{1,0:T(8,128)(2,1)S(1)}, bf16[128,1280]{1,0:T(8,128)(2,1)S(1)}, u32[]{:S(2)}, u32[]{:S(2)}) collective-permute-start(bf16[128,1280]{1,0:T(8,128)(2,1)S(1)} %get-tuple-element.57), channel_id=1, source_target_pairs={{0,8},{1,9},{2,10},{3,11},{4,12},{5,13},{6,14},{7,15},{8,0},{9,1},... | collective-permute-start | bytes 983048 | tf_op jit(solution)/shard_map/ppermute | solution.py:189
  458.4 7.3 %collective-permute-start.28 = (bf16[64,1280]{1,0:T(8,128)(2,1)S(1)}, bf16[64,1280]{1,0:T(8,128)(2,1)S(1)}, u32[]{:S(2)}, u32[]{:S(2)}) collective-permute-start(bf16[64,1280]{1,0:T(8,128)(2,1)S(1)} %select_convert_fusion.27), channel_id=1, source_target_pairs={{0,16},{1,17},{2,18},{3,19},{4,20},{5,21},{6,22},{7,23},{8,24},{9,... | collective-permute-start | bytes 491528 | tf_op jit(solution)/shard_map/ppermute | solution.py:189
  460.2 12.0 %collective-permute-start.12 = (bf16[128,1280]{1,0:T(8,128)(2,1)S(1)}, bf16[128,1280]{1,0:T(8,128)(2,1)S(1)}, u32[]{:S(2)}, u32[]{:S(2)}) collective-permute-start(bf16[128,1280]{1,0:T(8,128)(2,1)S(1)} %select_convert_fusion.9), channel_id=1, source_target_pairs={{0,16},{1,17},{2,18},{3,19},{4,20},{5,21},{6,22},{7,23},{8,24},{9,... | collective-permute-start | bytes 983048 | tf_op jit(solution)/shard_map/ppermute | solution.py:189
  466.0 8.3 %collective-permute-start.30 = (bf16[64,1280]{1,0:T(8,128)(2,1)S(1)}, bf16[64,1280]{1,0:T(8,128)(2,1)S(1)}, u32[]{:S(2)}, u32[]{:S(2)}) collective-permute-start(bf16[64,1280]{1,0:T(8,128)(2,1)S(1)} %get-tuple-element.59), channel_id=1, source_target_pairs={{0,8},{1,9},{2,10},{3,11},{4,12},{5,13},{6,14},{7,15},{8,0},{9,1},... | collective-permute-start | bytes 491528 | tf_op jit(solution)/shard_map/ppermute | solution.py:189
  468.9 38.3 %collective-permute-start.23 = (bf16[256,1280]{1,0:T(8,128)(2,1)}, bf16[256,1280]{1,0:T(8,128)(2,1)}, u32[]{:S(2)}, u32[]{:S(2)}) collective-permute-start(bf16[256,1280]{1,0:T(8,128)(2,1)} %pad_maximum_fusion.15), channel_id=1, source_target_pairs={{1,8},{3,10},{5,12},{7,14},{8,1},{10,3},{12,5},{14,7},{17,24},{19,... | collective-permute-start | bytes 1966088 | tf_op jit(solution)/shard_map/ppermute | solution.py:189
  472.8 26.8 %collective-permute-start.14 = (bf16[128,1280]{1,0:T(8,128)(2,1)S(1)}, bf16[128,1280]{1,0:T(8,128)(2,1)S(1)}, u32[]{:S(2)}, u32[]{:S(2)}) collective-permute-start(bf16[128,1280]{1,0:T(8,128)(2,1)S(1)} %get-tuple-element.53), channel_id=1, source_target_pairs={{0,8},{1,9},{2,10},{3,11},{4,12},{5,13},{6,14},{7,15},{8,0},{9,1},... | collective-permute-start | bytes 983048 | tf_op jit(solution)/shard_map/ppermute | solution.py:189
  475.1 29.0 %collective-permute-start.31 = (bf16[128,1280]{1,0:T(8,128)(2,1)}, bf16[128,1280]{1,0:T(8,128)(2,1)}, u32[]{:S(2)}, u32[]{:S(2)}) collective-permute-start(bf16[128,1280]{1,0:T(8,128)(2,1)} %pad_maximum_fusion.19), channel_id=1, source_target_pairs={{1,8},{3,10},{5,12},{7,14},{8,1},{10,3},{12,5},{14,7},{17,24},{19,... | collective-permute-start | bytes 983048 | tf_op jit(solution)/shard_map/ppermute | solution.py:189
  500.8 6.4 %collective-permute-start.15 = (bf16[256,1280]{1,0:T(8,128)(2,1)}, bf16[256,1280]{1,0:T(8,128)(2,1)}, u32[]{:S(2)}, u32[]{:S(2)}) collective-permute-start(bf16[256,1280]{1,0:T(8,128)(2,1)} %pad_maximum_fusion.12), channel_id=1, source_target_pairs={{1,8},{3,10},{5,12},{7,14},{8,1},{10,3},{12,5},{14,7},{17,24},{19,... | collective-permute-start | bytes 1966088 | tf_op jit(solution)/shard_map/ppermute | solution.py:189
  516.6 11.6 %collective-permute-start.42 = (bf16[1,1,4,128,640]{3,4,2,1,0:T(8,128)(2,1)}, bf16[1,1,4,128,640]{3,4,2,1,0:T(8,128)(2,1)}, u32[]{:S(2)}, u32[]{:S(2)}) collective-permute-start(bf16[1,1,4,128,640]{3,4,2,1,0:T(8,128)(2,1)} %bitcast.332), channel_id=1, source_target_pairs={{0,4},{1,5},{2,6},{3,7},{4,0},{5,1},{6,2},{7,3},{8,12},{9,13},{10,... | collective-permute-start | bytes 1966088 | tf_op jit(solution)/shard_map/ppermute | solution.py:189
  529.8 23.8 %collective-permute-start.45 = (bf16[128,640]{0,1:T(8,128)(2,1)S(1)}, bf16[128,640]{0,1:T(8,128)(2,1)S(1)}, u32[]{:S(2)}, u32[]{:S(2)}) collective-permute-start(bf16[128,640]{0,1:T(8,128)(2,1)S(1)} %pad_maximum_fusion.26), channel_id=1, source_target_pairs={{0,16},{1,17},{2,18},{3,19},{4,20},{5,21},{6,22},{7,23},{8,24},{9,... | collective-permute-start | bytes 491528 | tf_op jit(solution)/shard_map/ppermute | solution.py:189
  531.8 21.0 %collective-permute-start.33 = (bf16[128,640]{0,1:T(8,128)(2,1)S(1)}, bf16[128,640]{0,1:T(8,128)(2,1)S(1)}, u32[]{:S(2)}, u32[]{:S(2)}) collective-permute-start(bf16[128,640]{0,1:T(8,128)(2,1)S(1)} %pad_maximum_fusion.22), channel_id=1, source_target_pairs={{0,8},{1,9},{2,10},{3,11},{4,12},{5,13},{6,14},{7,15},{8,0},{9,1},... | collective-permute-start | bytes 491528 | tf_op jit(solution)/shard_map/ppermute | solution.py:189
  547.9 7.6 %collective-permute-start.43 = (bf16[128,640]{0,1:T(8,128)(2,1)S(1)}, bf16[128,640]{0,1:T(8,128)(2,1)S(1)}, u32[]{:S(2)}, u32[]{:S(2)}) collective-permute-start(bf16[128,640]{0,1:T(8,128)(2,1)S(1)} %pad_maximum_fusion.25), channel_id=1, source_target_pairs={{0,8},{1,9},{2,10},{3,11},{4,12},{5,13},{6,14},{7,15},{8,0},{9,1},... | collective-permute-start | bytes 491528 | tf_op jit(solution)/shard_map/ppermute | solution.py:189
  548.1 10.3 %collective-permute-start.35 = (bf16[128,640]{0,1:T(8,128)(2,1)S(1)}, bf16[128,640]{0,1:T(8,128)(2,1)S(1)}, u32[]{:S(2)}, u32[]{:S(2)}) collective-permute-start(bf16[128,640]{0,1:T(8,128)(2,1)S(1)} %pad_maximum_fusion.23), channel_id=1, source_target_pairs={{0,16},{1,17},{2,18},{3,19},{4,20},{5,21},{6,22},{7,23},{8,24},{9,... | collective-permute-start | bytes 491528 | tf_op jit(solution)/shard_map/ppermute | solution.py:189
  556.7 6.9 %collective-permute-start.46 = (bf16[64,640]{0,1:T(8,128)(2,1)S(1)}, bf16[64,640]{0,1:T(8,128)(2,1)S(1)}, u32[]{:S(2)}, u32[]{:S(2)}) collective-permute-start(bf16[64,640]{0,1:T(8,128)(2,1)S(1)} %get-tuple-element.87), channel_id=1, source_target_pairs={{0,8},{1,9},{2,10},{3,11},{4,12},{5,13},{6,14},{7,15},{8,0},{9,1},... | collective-permute-start | bytes 245768 | tf_op jit(solution)/shard_map/ppermute | solution.py:189
  559.3 6.7 %collective-permute-start.36 = (bf16[64,640]{0,1:T(8,128)(2,1)S(1)}, bf16[64,640]{0,1:T(8,128)(2,1)S(1)}, u32[]{:S(2)}, u32[]{:S(2)}) collective-permute-start(bf16[64,640]{0,1:T(8,128)(2,1)S(1)} %get-tuple-element.93), channel_id=1, source_target_pairs={{0,8},{1,9},{2,10},{3,11},{4,12},{5,13},{6,14},{7,15},{8,0},{9,1},... | collective-permute-start | bytes 245768 | tf_op jit(solution)/shard_map/ppermute | solution.py:189
  564.2 7.1 %collective-permute-start.47 = (bf16[128,640]{0,1:T(8,128)(2,1)S(1)}, bf16[128,640]{0,1:T(8,128)(2,1)}, u32[]{:S(2)}, u32[]{:S(2)}) collective-permute-start(bf16[128,640]{0,1:T(8,128)(2,1)S(1)} %pad_maximum_fusion.27), channel_id=1, source_target_pairs={{0,1},{1,0},{2,3},{3,2},{4,5},{5,4},{6,7},{7,6},{8,9},{9,8},{10,11... | collective-permute-start | bytes 491528 | tf_op jit(solution)/shard_map/ppermute | solution.py:189
  570.6 8.4 %collective-permute-start.48 = (bf16[128,640]{0,1:T(8,128)(2,1)S(1)}, bf16[128,640]{0,1:T(8,128)(2,1)S(1)}, u32[]{:S(2)}, u32[]{:S(2)}) collective-permute-start(bf16[128,640]{0,1:T(8,128)(2,1)S(1)} %pad_maximum_fusion.27), channel_id=1, source_target_pairs={{1,2},{2,1},{5,6},{6,5},{9,10},{10,9},{13,14},{14,13},{17,18},{18,... | collective-permute-start | bytes 491528 | tf_op jit(solution)/shard_map/ppermute | solution.py:189
  571.3 9.7 %collective-permute-start.50 = (bf16[128,640]{0,1:T(8,128)(2,1)}, bf16[128,640]{0,1:T(8,128)(2,1)S(1)}, u32[]{:S(2)}, u32[]{:S(2)}) collective-permute-start(bf16[128,640]{0,1:T(8,128)(2,1)} %collective-permute-done.47), channel_id=1, source_target_pairs={{1,2},{2,1},{5,6},{6,5},{9,10},{10,9},{13,14},{14,13},{17,18},{18,... | collective-permute-start | bytes 491528 | tf_op jit(solution)/shard_map/ppermute | solution.py:189
  573.8 8.5 %collective-permute-start.40 = (bf16[128,640]{0,1:T(8,128)(2,1)S(1)}, bf16[128,640]{0,1:T(8,128)(2,1)S(1)}, u32[]{:S(2)}, u32[]{:S(2)}) collective-permute-start(bf16[128,640]{0,1:T(8,128)(2,1)S(1)} %collective-permute-done.37), channel_id=1, source_target_pairs={{1,2},{2,1},{5,6},{6,5},{9,10},{10,9},{13,14},{14,13},{17,18},{18,... | collective-permute-start | bytes 491528 | tf_op jit(solution)/shard_map/ppermute | solution.py:189
  574.4 14.0 %collective-permute-start.39 = (bf16[128,640]{0,1:T(8,128)(2,1)S(1)}, bf16[128,640]{0,1:T(8,128)(2,1)S(1)}, u32[]{:S(2)}, u32[]{:S(2)}) collective-permute-start(bf16[128,640]{0,1:T(8,128)(2,1)S(1)} %collective-permute-done.38), channel_id=1, source_target_pairs={{1,0},{2,3},{5,4},{6,7},{9,8},{10,11},{13,12},{14,15},{17,16},{18,... | collective-permute-start | bytes 491528 | tf_op jit(solution)/shard_map/ppermute | solution.py:189
  579.0 22.1 %collective-permute-start.49 = (bf16[128,640]{0,1:T(8,128)(2,1)S(1)}, bf16[128,640]{0,1:T(8,128)(2,1)S(1)}, u32[]{:S(2)}, u32[]{:S(2)}) collective-permute-start(bf16[128,640]{0,1:T(8,128)(2,1)S(1)} %collective-permute-done.48), channel_id=1, source_target_pairs={{1,0},{2,3},{5,4},{6,7},{9,8},{10,11},{13,12},{14,15},{17,16},{18,... | collective-permute-start | bytes 491528 | tf_op jit(solution)/shard_map/ppermute | solution.py:189
  581.0 21.5 %collective-permute-start.51 = (bf16[128,640]{0,1:T(8,128)(2,1)S(1)}, bf16[128,640]{0,1:T(8,128)(2,1)S(1)}, u32[]{:S(2)}, u32[]{:S(2)}) collective-permute-start(bf16[128,640]{0,1:T(8,128)(2,1)S(1)} %collective-permute-done.50), channel_id=1, source_target_pairs={{1,0},{2,3},{5,4},{6,7},{9,8},{10,11},{13,12},{14,15},{17,16},{18,... | collective-permute-start | bytes 491528 | tf_op jit(solution)/shard_map/ppermute | solution.py:189
  582.3 15.1 %collective-permute-start.41 = (bf16[128,640]{0,1:T(8,128)(2,1)S(1)}, bf16[128,640]{0,1:T(8,128)(2,1)S(1)}, u32[]{:S(2)}, u32[]{:S(2)}) collective-permute-start(bf16[128,640]{0,1:T(8,128)(2,1)S(1)} %collective-permute-done.40), channel_id=1, source_target_pairs={{1,0},{2,3},{5,4},{6,7},{9,8},{10,11},{13,12},{14,15},{17,16},{18,... | collective-permute-start | bytes 491528 | tf_op jit(solution)/shard_map/ppermute | solution.py:189
  (45 other events, 369.0 us)
